TPU v7x, 256 devices: a whole 4x4x8 slice. The times are simulated.
256 devices in a mesh: dp: 64 (over x, z, core), tensor: 4 (over y).
Axes of the slice: x: 4, y: 4, z: 8, core: 2. Of those that a mesh axis runs over, the one named last changes fastest.
Arguments:
- gate_preactivation: bfloat16 [1024, 28672], P('dp', 'tensor'), may hold values from -6 to 6
- up_preactivation: bfloat16 [1024, 28672], P('dp', 'tensor'), may hold values from -6 to 6
- cotangent: bfloat16 [1024, 8192], P('dp'), may hold values from -0.1875 to 0.1875
- down_weight: bfloat16 [28672, 8192], P('tensor', 'dp'), may hold values from -0.03125 to 0.03125
- lowrank_factor_first: bfloat16 [28672, 64], P('tensor'), may hold values from -0.03125 to 0.03125
- lowrank_factor_second: bfloat16 [64, 8192], replicated, may hold values from -0.75 to 0.75
- sparse_block_values: bfloat16 [64, 4, 2, 128, 128], P('dp', 'tensor'), may hold values from -0.5 to 0.5
- slot_block_rows: int32 [64, 4, 2], P(None, 'tensor'), may hold values from 0 to 55, as said below
- slot_block_columns: int32 [64, 4, 2], P(None, 'tensor'), may hold values from 0 to 0
- owner_slot_counts: int32 [64, 4], P(None, 'tensor'), may hold values from 1 to 2, as said below
Outputs:
- mixed: bfloat16 [1024, 8192], P('tensor', 'dp')
- grad_a: float32 [28672, 64], P('tensor')
- grad_b: float32 [64, 8192], P(None, 'dp')
- grad_blocks: float32 [64, 4, 2, 128, 128], P('dp', 'tensor')
Inputs may be any that keep to these rules, and one draw needn't show every extreme that they name: `slot_block_rows`: the 2 slots of one owner name different blocks. `owner_slot_counts`: some owner has exactly 2 live slots.
All inputs are finite; a program needn't handle non-finite values.
Results may differ from a plain program's by a relative error of at most 0.0049.
Values may be sent and summed in bfloat16 or wider, within the bound.
No kernel may reach another device: no remote copies, remote signals or barrier semaphores. Data moves between devices by JAX's collectives and lax.ppermute only.
A program may use at most 128 MiB of HBM per device.

v0:
```python
import jax
import jax.numpy as jnp
from jax import lax
from jax.sharding import Mesh
from jax.sharding import PartitionSpec as P

DP = ("dp_0", "dp_1", "dp_2")


def split_up(array, dim, count):
    before, after = (array.shape[:dim], array.shape[dim + 1 :])
    return jnp.moveaxis(array.reshape(*before, count, -1, *after), dim, 0)


def sent_and_summed(array, axis, dim):
    blocks = split_up(array, dim, lax.axis_size(axis))
    arrived = lax.all_to_all(blocks, axis, split_axis=0, concat_axis=0, tiled=True)
    return arrived.sum(axis=0)


def sent_to_all(array, axis):
    count = lax.axis_size(axis)
    return lax.all_to_all(
        jnp.broadcast_to(array[None], (count, *array.shape)), axis, 0, 0, tiled=True
    )


def of_everyone(array, axis):
    return sent_to_all(array, axis).sum(axis=0)


def joined_along(blocks, dim):
    blocks = jnp.moveaxis(blocks, 0, dim)
    lengths = blocks.shape
    return blocks.reshape(*lengths[:dim], lengths[dim] * lengths[dim + 1], *lengths[dim + 2 :])


def collect(array, axis, dim):
    return joined_along(sent_to_all(array, axis), dim)


def all_blocks(array, axes, turns):
    blocks = array
    for k in turns:
        blocks = lax.all_gather(blocks, axes[k])
    done = turns[::-1]
    back = [done.index(k) for k in range(len(axes))]
    blocks = blocks.transpose(*back, *range(len(axes), blocks.ndim))
    return blocks.reshape(-1, *array.shape)


def gathered_by_axis(array, axes, turns, dim):
    return joined_along(all_blocks(array, axes, turns), dim)


def column_view(cotangent):
    return lax.all_to_all(cotangent, DP, split_axis=1, concat_axis=0, tiled=True)


def shards(
    gate_preactivation,
    up_preactivation,
    cotangent,
    down_weight,
    lowrank_factor_first,
    lowrank_factor_second,
    sparse_block_values,
    slot_block_rows,
    slot_block_columns,
    owner_slot_counts,
):
    data_parallel_index = lax.axis_index(DP)
    column_offset = down_weight.shape[1]
    side = sparse_block_values.shape[-1]
    slots = sparse_block_values.shape[2]
    per_col = column_offset // side
    hidden_activation = (
        jax.nn.silu(gate_preactivation.astype(jnp.float32)) * up_preactivation.astype(jnp.float32)
    ).astype(jnp.bfloat16)
    hidden_gathered = lax.all_gather(hidden_activation, DP, axis=0, tiled=True)
    tok_all = hidden_gathered.shape[0]
    rows_all = slot_block_rows[:, 0, :]
    cols_all = slot_block_columns[:, 0, :]
    live_all = (
        jnp.arange(slots, dtype=jnp.int32)[None, :] < owner_slot_counts[:, 0][:, None]
    ).astype(jnp.float32)
    own_rows = lax.dynamic_index_in_dim(rows_all, data_parallel_index, 0, keepdims=False)
    own_cols = lax.dynamic_index_in_dim(cols_all, data_parallel_index, 0, keepdims=False)
    own_live = lax.dynamic_index_in_dim(live_all, data_parallel_index, 0, keepdims=False)
    factor_b_window = lax.dynamic_slice_in_dim(
        lowrank_factor_second, data_parallel_index * column_offset, column_offset, 1
    ).astype(jnp.float32)
    col_pick = (own_cols[:, None] == jnp.arange(per_col, dtype=jnp.int32)[None, :]).astype(
        jnp.float32
    ) * own_live[:, None]
    blocks = sparse_block_values[0, 0]
    owned_hidden = jnp.stack(
        [
            lax.dynamic_slice_in_dim(hidden_gathered, own_rows[slot] * side, side, 1)
            for slot in range(slots)
        ],
        axis=1,
    )
    total = jnp.dot(hidden_gathered, down_weight, preferred_element_type=jnp.float32)
    lowrank_token_rows = jnp.dot(
        hidden_gathered, lowrank_factor_first, preferred_element_type=jnp.float32
    )
    total = total + jnp.dot(lowrank_token_rows, factor_b_window, precision=lax.Precision.HIGHEST)
    local = jnp.einsum("tkc,kcd->tkd", owned_hidden, blocks, preferred_element_type=jnp.float32)
    spread = jnp.einsum("tkd,kn->tnd", local, col_pick, precision=lax.Precision.HIGHEST)
    summed = sent_and_summed(
        total
        + spread.reshape(
            tok_all // lax.axis_size("tensor") * lax.axis_size("tensor"), column_offset
        ),
        "tensor",
        0,
    )
    mixed = summed.astype(jnp.bfloat16)
    cotangent_lowrank = lax.dot_general(
        cotangent,
        lowrank_factor_second,
        (((1,), (1,)), ((), ())),
        preferred_element_type=jnp.float32,
    ).astype(jnp.bfloat16)
    lowrank_local_part = jnp.dot(
        hidden_activation, lowrank_factor_first, preferred_element_type=jnp.float32
    )
    cot_cols = None
    cot_cols = column_view(cotangent)
    low_full = of_everyone(lowrank_local_part, "tensor")
    low_all = collect(low_full, DP, 0)
    grad_b = lax.dot_general(
        low_all,
        cot_cols.astype(jnp.float32),
        (((0,), (0,)), ((), ())),
        precision=lax.Precision.HIGHEST,
    )
    cot_all = gathered_by_axis(cotangent_lowrank, DP, (0, 1, 2), 0)
    grad_a = lax.dot_general(
        hidden_gathered, cot_all, (((0,), (0,)), ((), ())), preferred_element_type=jnp.float32
    )
    pick_own = (own_cols[:, None] == jnp.arange(per_col, dtype=jnp.int32)[None, :]).astype(
        jnp.bfloat16
    )
    picked_c = jnp.einsum(
        "tnd,kn->tkd",
        cot_cols.reshape(tok_all, per_col, side),
        pick_own,
        preferred_element_type=jnp.float32,
    ).astype(jnp.bfloat16)
    owned = jnp.einsum("tkc,tkd->kcd", owned_hidden, picked_c, preferred_element_type=jnp.float32)
    grad_blocks = (owned * own_live[:, None, None])[None, None]
    return (mixed, grad_a, grad_b, grad_blocks)


def solution(mesh):
    finer = Mesh(
        mesh.devices.reshape(4, 8, 2, mesh.shape["tensor"]), ("dp_0", "dp_1", "dp_2", "tensor")
    )
    in_specs = (
        P(DP, "tensor"),
        P(DP, "tensor"),
        P(DP, None),
        P("tensor", DP),
        P("tensor", None),
        P(),
        P(DP, "tensor", None, None, None),
        P(None, "tensor", None),
        P(None, "tensor", None),
        P(None, "tensor"),
    )
    out_specs = (P("tensor", DP), P("tensor", None), P(None, DP), P(DP, "tensor", None, None, None))
    return jax.shard_map(
        shards, mesh=finer, in_specs=in_specs, out_specs=out_specs, check_vma=False
    )
```

profile of v0, /device:TPU:1, one launch (start us, length us, event | category | flops | bytes accessed | tf_op | source)
XLA Modules:
  0.0 160.6 jit_solution(10013752832817767674)
XLA Ops:
  7.2 0.0 copy-start
  7.2 0.0 copy-start.2
  7.2 0.0 all-gather.5.cloned.1.call-start
  7.2 2.1 %fusion.12 = bf16[16,7168]{1,0:T(8,128)(2,1)} fusion(bf16[16,7168]{1,0:T(8,128)(2,1)} %param.11, bf16[16,7168]{1,0:T(8,128)(2,1)} %param.10), kind=kLoop, calls=%fused_computation.20 | loop fusion | flops 917504 | bytes 688128 | tf_op jit(solution)/shard_map/convert_element_type | solution.py:79
  9.3 0.0 all-gather.5.cloned.1.call-update
  9.3 1.6 %fusion.27 = f32[16,64]{1,0:T(8,128)S(1)} fusion(bf16[16,7168]{1,0:T(8,128)(2,1)} %fusion.12, bf16[7168,64]{0,1:T(8,128)(2,1)} %param.14), kind=kOutput, calls=%fused_computation.43 | convolution fusion | flops 14680064 | bytes 1150976 | tf_op jit(solution)/shard_map/dot_general | solution.py:126
  11.0 0.7 reshape.70
  11.7 5.0 %all-to-all-start.1 = ((f32[4,1,1024]{2,1,0:T(1,128)}), f32[4,1,1024]{2,1,0:T(1,128)S(1)}, u32[]{:S(2)}, u32[]{:S(2)}) async-start(f32[4,1,1024]{2,1,0:T(1,128)} %reshape.70), calls=%async_computation.1 | async-start | bytes 32768 | tf_op jit(solution)/shard_map/all_to_all | solution.py:23
  16.7 1.7 %copy_bitcast_fusion = bf16[16,64,128]{2,0,1:T(8,128)(2,1)} fusion(bf16[16,8192]{1,0:T(8,128)(2,1)} %param.12), kind=kLoop, calls=%fused_computation.21 | loop fusion | bytes 524288 | tf_op jit(solution)/shard_map/all_to_all | solution.py:57
  18.4 2.5 %all-to-all-done.1 = f32[4,1,1024]{2,1,0:T(1,128)S(1)} async-done(((f32[4,1,1024]{2,1,0:T(1,128)}), f32[4,1,1024]{2,1,0:T(1,128)S(1)}, u32[]{:S(2)}, u32[]{:S(2)}) %all-to-all-start.1) | async-done | bytes 16416 | tf_op jit(solution)/shard_map/all_to_all | solution.py:23
  20.9 13.6 %all-to-all-start.3 = ((bf16[16,64,128]{2,0,1:T(8,128)(2,1)}), bf16[16,64,128]{2,0,1:T(8,128)(2,1)S(1)}, u32[]{:S(2)}, u32[]{:S(2)}) async-start(bf16[16,64,128]{2,0,1:T(8,128)(2,1)} %copy_bitcast_fusion), calls=%async_computation.3 | async-start | bytes 524288 | tf_op jit(solution)/shard_map/all_to_all | solution.py:57
  34.5 0.8 constant_dynamic-slice_fusion
  35.3 1.7 %convolution_convert_fusion = bf16[16,64]{1,0:T(8,128)(2,1)S(1)} fusion(bf16[16,8192]{1,0:T(8,128)(2,1)} %param.12, bf16[64,8192]{1,0:T(8,128)(2,1)} %param.15), kind=kOutput, calls=%fused_computation.6 | convolution fusion | flops 16778240 | bytes 1312768 | tf_op jit(solution)/shard_map/dot_general | solution.py:120
  36.9 0.6 broadcast.31
  37.5 0.7 reduce.2
  38.2 0.1 reshape.71
  38.4 1.0 reshape.72
  39.4 9.2 %all-to-all-done.3 = bf16[16,64,128]{2,0,1:T(8,128)(2,1)S(1)} async-done(((bf16[16,64,128]{2,0,1:T(8,128)(2,1)}), bf16[16,64,128]{2,0,1:T(8,128)(2,1)S(1)}, u32[]{:S(2)}, u32[]{:S(2)}) %all-to-all-start.3) | async-done | bytes 262176 | tf_op jit(solution)/shard_map/all_to_all | solution.py:57
  48.6 6.4 %all-to-all-start.2 = ((f32[64,1,1024]{2,1,0:T(1,128)}), f32[64,1,1024]{2,1,0:T(1,128)}, u32[]{:S(2)}, u32[]{:S(2)}) async-start(f32[64,1,1024]{2,1,0:T(1,128)} %reshape.72), calls=%async_computation.2 | async-start | bytes 524288 | tf_op jit(solution)/shard_map/all_to_all | solution.py:23
  55.0 0.5 fusion.23
  56.8 1.2 dynamic-slice.2
  58.1 0.9 compare_reduce_fusion
  58.9 10.5 %all-gather = bf16[64,64]{1,0:T(8,128)(2,1)S(1)} all-gather(bf16[16,64]{1,0:T(8,128)(2,1)S(1)} %convolution_convert_fusion), channel_id=2, replica_groups=mesh['dp_0'=4,'dp_1'=8,'dp_2'=2,'tensor'=4] {'dp_0'}, dimensions={0}, use_global_device_ids=true | all-gather | bytes 10240 | tf_op jit(solution)/shard_map/all_gather | solution.py:45
  69.4 22.0 %all-gather.1 = bf16[32,16,64]{2,1,0:T(8,128)(2,1)S(1)} all-gather(bf16[4,16,64]{2,1,0:T(8,128)(2,1)S(1)} %bitcast.65), channel_id=3, replica_groups=mesh['dp_0'=4,'dp_1'=8,'dp_2'=2,'tensor'=4] {'dp_1'}, dimensions={0}, use_global_device_ids=true | all-gather | bytes 73728 | tf_op jit(solution)/shard_map/all_gather | solution.py:45
  91.3 8.6 %all-gather.2 = bf16[16,4,16,64]{3,2,1,0:T(8,128)(2,1)S(1)} all-gather(bf16[8,4,16,64]{3,2,1,0:T(8,128)(2,1)S(1)} %bitcast.63), channel_id=4, replica_groups=mesh['dp_0'=4,'dp_1'=8,'dp_2'=2,'tensor'=4] {'dp_2'}, dimensions={0}, use_global_device_ids=true | all-gather | bytes 196608 | tf_op jit(solution)/shard_map/all_gather | solution.py:45
  100.0 0.7 fusion.17
  100.7 0.9 bitcast_convert_fusion
  101.5 0.0 all-to-all-done.2
  101.6 2.2 %reduce.3 = f32[64,1024]{1,0:T(8,128)S(1)} reduce(f32[64,1,1024]{2,1,0:T(1,128)} %all-to-all-done.2, f32[]{:T(128)} %broadcast.31), dimensions={1}, to_apply=%all_to_all.23.reduce_sub_computation | reduce | bytes 524292 | tf_op jit(solution)/shard_map/all_to_all | solution.py:23
  103.8 0.9 reshape.73
  104.7 2.2 %convolution_bitcast_fusion.1 = f32[64,128]{1,0:T(8,128)} fusion(f32[64,16,64]{2,1,0:T(8,128)} %reshape.73, bf16[16,64,128]{2,0,1:T(8,128)(2,1)S(1)} %all-to-all-done.3), kind=kOutput, calls=%fused_computation.5 | convolution fusion | flops 100663296 | bytes 557056 | tf_op jit(solution)/shard_map/dot_general | solution.py:133
  107.0 5.6 %all-gather.5.cloned.1.call-done = bf16[1024,7168]{1,0:T(8,128)(2,1)} async-done(((bf16[16,7168]{1,0:T(8,128)(2,1)}), bf16[1024,7168]{1,0:T(8,128)(2,1)}) %all-gather.5.cloned.1.call-update) | async-done | bytes 14680080 | tf_op jit(solution)/shard_map/all_gather | solution.py:80
  112.6 0.0 copy-start.1
  112.6 1.2 dynamic-slice_bitcast_fusion.1
  113.8 1.3 convolution_bitcast_fusion
  115.2 7.9 %fusion.2 = f32[1,1024,128]{2,0,1:T(1,128)S(1)} fusion(f32[1024,2,128]{2,0,1:T(8,128)S(1)} %convolution_bitcast_fusion, pred[2]{0:T(512)(128)(4,1)S(1)} %compare_reduce_fusion, s32[1]{0:T(128)} %dynamic-slice.2), kind=kOutput, calls=%fused_computation.8 | convolution fusion | flops 3145734 | bytes 1572870 | tf_op jit(solution)/shard_map/tkd,kn->tnd/dot_general | solution.py:110
  123.1 0.0 copy-done.2
  123.1 9.7 %fusion.25 = f32[1024,64]{0,1:T(8,128)S(1)} fusion(bf16[1024,7168]{1,0:T(8,128)(2,1)} %all-gather.5.cloned.1.call-done, bf16[7168,64]{0,1:T(8,128)(2,1)S(1)} %copy-done.2), kind=kOutput, calls=%fused_computation.41 | convolution fusion | flops 939524096 | bytes 15859712 | tf_op jit(solution)/shard_map/dot_general | solution.py:105
  132.8 0.0 copy-done
  132.8 0.0 copy-done.1
  132.8 4.0 %fusion.24 = f32[1024,128]{1,0:T(8,128)S(1)} fusion(bf16[1024,7168]{1,0:T(8,128)(2,1)S(1)} %copy-done.1, bf16[7168,128]{1,0:T(8,128)(2,1)S(1)} %copy-done), kind=kOutput, calls=%fused_computation.40 | convolution fusion | flops 1879048192 | bytes 17039360 | tf_op jit(solution)/shard_map/dot_general | solution.py:104
  136.8 2.2 %fusion = f32[1024,128]{1,0:T(8,128)} fusion(f32[1024,128]{1,0:T(8,128)S(1)} %bitcast.64, f32[1024,128]{1,0:T(8,128)S(1)} %fusion.24, f32[1024,64]{0,1:T(8,128)S(1)} %fusion.25, bf16[64,8192]{1,0:T(8,128)(2,1)} %param.15, s32[]{:T(128)S(6)} %select_n.16), kind=kOutput, calls=%fused_computation.2 | convolution fusion | flops 100925440 | bytes 1851396 | tf_op jit(solution)/shard_map/dot_general | solution.py:108
  138.9 3.9 %all-to-all-start = ((f32[4,256,128]{2,1,0:T(8,128)}), f32[4,256,128]{2,1,0:T(8,128)S(1)}, u32[]{:S(2)}, u32[]{:S(2)}) async-start(f32[4,256,128]{2,1,0:T(8,128)} %bitcast.12), calls=%async_computation | async-start | bytes 1048576 | tf_op jit(solution)/shard_map/all_to_all | solution.py:17
  142.9 0.0 copy-start.3
  142.9 9.2 %fusion.26 = f32[7168,64]{0,1:T(8,128)} fusion(bf16[1024,7168]{1,0:T(8,128)(2,1)} %all-gather.5.cloned.1.call-done, bf16[1024,64]{1,0:T(8,128)(2,1)S(1)} %bitcast.61), kind=kOutput, calls=%fused_computation.42 | convolution fusion | flops 939524096 | bytes 16646144 | tf_op jit(solution)/shard_map/dot_general | solution.py:140
  152.1 0.0 copy-done.3
  152.1 1.0 fusion.1
  153.1 0.0 all-to-all-done
  153.1 0.7 reduce_sum.18
  (5 shorter events, 0.1 us)
Async XLA Ops:
  7.2 125.6 %copy-start = (bf16[7168,128]{1,0:T(8,128)(2,1)S(1)}, bf16[7168,128]{1,0:T(8,128)(2,1)}, u32[]{:S(2)}) copy-start(bf16[7168,128]{1,0:T(8,128)(2,1)} %param.13) | copy-start | bytes 5505028
  7.2 115.9 %copy-start.2 = (bf16[7168,64]{0,1:T(8,128)(2,1)S(1)}, bf16[7168,64]{0,1:T(8,128)(2,1)}, u32[]{:S(2)}) copy-start(bf16[7168,64]{0,1:T(8,128)(2,1)} %param.14) | copy-start | bytes 2752516
  7.2 105.4 %all-gather.5.cloned.1.call-start = ((), (), s32[]{:S(2)}) async-start(), calls=%async_computation.4 | async-start | bytes 14909440 | tf_op jit(solution)/shard_map/all_gather | solution.py:80
  11.7 9.2 %all-to-all-start.1 = ((f32[4,1,1024]{2,1,0:T(1,128)}), f32[4,1,1024]{2,1,0:T(1,128)S(1)}, u32[]{:S(2)}, u32[]{:S(2)}) async-start(f32[4,1,1024]{2,1,0:T(1,128)} %reshape.70), calls=%async_computation.1 | async-start | bytes 32768 | tf_op jit(solution)/shard_map/all_to_all | solution.py:23
  20.9 27.7 %all-to-all-start.3 = ((bf16[16,64,128]{2,0,1:T(8,128)(2,1)}), bf16[16,64,128]{2,0,1:T(8,128)(2,1)S(1)}, u32[]{:S(2)}, u32[]{:S(2)}) async-start(bf16[16,64,128]{2,0,1:T(8,128)(2,1)} %copy_bitcast_fusion), calls=%async_computation.3 | async-start | bytes 524288 | tf_op jit(solution)/shard_map/all_to_all | solution.py:57
  48.6 53.0 %all-to-all-start.2 = ((f32[64,1,1024]{2,1,0:T(1,128)}), f32[64,1,1024]{2,1,0:T(1,128)}, u32[]{:S(2)}, u32[]{:S(2)}) async-start(f32[64,1,1024]{2,1,0:T(1,128)} %reshape.72), calls=%async_computation.2 | async-start | bytes 524288 | tf_op jit(solution)/shard_map/all_to_all | solution.py:23
  112.6 20.2 %copy-start.1 = (bf16[1024,7168]{1,0:T(8,128)(2,1)S(1)}, bf16[1024,7168]{1,0:T(8,128)(2,1)}, u32[]{:S(2)}) copy-start(bf16[1024,7168]{1,0:T(8,128)(2,1)} %all-gather.5.cloned.1.call-done) | copy-start | bytes 44040196
  138.9 14.2 %all-to-all-start = ((f32[4,256,128]{2,1,0:T(8,128)}), f32[4,256,128]{2,1,0:T(8,128)S(1)}, u32[]{:S(2)}, u32[]{:S(2)}) async-start(f32[4,256,128]{2,1,0:T(8,128)} %bitcast.12), calls=%async_computation | async-start | bytes 1048576 | tf_op jit(solution)/shard_map/all_to_all | solution.py:17
  142.9 9.2 %copy-start.3 = (f32[1024,128]{1,0:T(8,128)S(1)}, f32[1024,128]{1,0:T(8,128)}, u32[]{:S(2)}) copy-start(f32[1024,128]{1,0:T(8,128)} %bitcast_convert_fusion) | copy-start | bytes 1572868
Sparse Core Ops, SparseCore 0:
  10.7 101.7 all-gather.4
where the time goes:
time: 161 us
  blocking collectives  41 us (25%)
  matrix products  40.9 us (25%)
  starting transfers between devices  29 us (18%)
  waiting for transfers between devices  17.4 us (11%)
  between operations  15.5 us (10%)
  local copies, waits for them, and re-layouts  8.89 us (6%)
  other arithmetic  8 us (5%)
    all_gather x3, blocking collectives, all_blocks(): blocks = lax.all_gather(blocks, axes[k])  41 us
    all_to_all x1, starting transfers between devices, column_view(): lax.all_to_all(cotangent, DP, split_axis=1, concat_axis=0, tiled=True)  13.6 us
    all_to_all x2, starting transfers between devices, sent_to_all(): lax.all_to_all(jnp.broadcast_to(array[None], (count, *array.shape)), axis...  11.4 us
    dot_general x1, matrix products, shards(): jnp.dot(hidden_gathered, lowrank_factor_first, preferred_element_type=jnp...  9.72 us
    all_to_all x1, waiting for transfers between devices, column_view(): lax.all_to_all(cotangent, DP, split_axis=1, concat_axis=0, tiled=True)  9.2 us
    dot_general x1, matrix products, shards(): lax.dot_general(hidden_gathered, cot_all, (((0,), (0,)), ((), ())), prefe...  9.19 us
    dot_general x1, matrix products, shards(): jnp.einsum('tkd,kn->tnd', local, col_pick, precision=lax.Precision.HIGHEST)  7.9 us
    all_gather x1, waiting for transfers between devices, shards(): hidden_gathered = lax.all_gather(hidden_activation, DP, axis=0, tiled=True)  5.64 us
  transfers between devices with their start and end apart: 5, of which 3 were waited for; matrix products, arithmetic and copies ran while one was open for 18% of the time, Pallas kernels for 0%

commit v1 on v0

--- a/solution.py
+++ b/solution.py
@@ -77,7 +77,10 @@
     hidden_activation = (
         jax.nn.silu(gate_preactivation.astype(jnp.float32)) * up_preactivation.astype(jnp.float32)
     ).astype(jnp.bfloat16)
-    hidden_gathered = lax.all_gather(hidden_activation, DP, axis=0, tiled=True)
+    f_next = jax.lax.all_to_all(
+        jnp.stack([hidden_activation for _ in range(jax.lax.axis_size(DP))]), DP, 0, 0
+    )
+    hidden_gathered = jnp.concatenate(f_next, 0)
     tok_all = hidden_gathered.shape[0]
     rows_all = slot_block_rows[:, 0, :]
     cols_all = slot_block_columns[:, 0, :]

time: 161 us -> 460 us (2.86)
  blocking collectives: 41 us -> 353 us
  between operations: 15.5 us -> 2.13 us
  local copies, waits for them, and re-layouts: 8.89 us -> 13.7 us
  waiting for transfers between devices: 17.4 us -> 12.7 us
    all_gather x3, blocking collectives: 41 us -> 335 us  [all_blocks(): blocks = lax.all_gather(blocks, axes[k])]
    all_to_all x0 -> x1, blocking collectives: none -> 17.9 us  [sent_to_all(): lax.all_to_all(jnp.broadcast_to(array[None], (count, *array.shape)), axis...]
    another operation x0 -> x1, local copies, waits for them, and re-layouts: none -> 7.01 us  [shards(): jnp.stack([hidden_activation for _ in range(jax.lax.axis_size(DP))])]
    all_to_all x2 -> x1, starting transfers between devices: 11.4 us -> 5 us  [sent_to_all(): lax.all_to_all(jnp.broadcast_to(array[None], (count, *array.shape)), axis...]
    all_to_all x0 -> x1, starting transfers between devices: none -> 6.34 us  [shards(): jax.lax.all_to_all(jnp.stack([hidden_activation for _ in range(jax.lax.ax...]
    all_gather x1 -> x0, waiting for transfers between devices: 5.64 us -> none  [shards(): hidden_gathered = lax.all_gather(hidden_activation, DP, axis=0, tiled=True)]
  transfers between devices with their start and end apart: 5 -> 4, of which waited for: 3 -> 2; matrix products, arithmetic and copies ran while one was open for 18% -> 5% of each run, Pallas kernels for 0% -> 0%
where the time goes in v1:
time: 460 us
  blocking collectives  353 us (77%)
  matrix products  42.5 us (9%)
  starting transfers between devices  28.6 us (6%)
  local copies, waits for them, and re-layouts  13.7 us (3%)
  waiting for transfers between devices  12.7 us (3%)
  other arithmetic  6.66 us (1%)
    all_gather x3, blocking collectives, all_blocks(): blocks = lax.all_gather(blocks, axes[k])  335 us
    all_to_all x1, blocking collectives, sent_to_all(): lax.all_to_all(jnp.broadcast_to(array[None], (count, *array.shape)), axis...  17.9 us
    all_to_all x1, starting transfers between devices, column_view(): lax.all_to_all(cotangent, DP, split_axis=1, concat_axis=0, tiled=True)  13.6 us
    all_to_all x1, waiting for transfers between devices, column_view(): lax.all_to_all(cotangent, DP, split_axis=1, concat_axis=0, tiled=True)  10.2 us
    dot_general x1, matrix products, shards(): jnp.dot(hidden_gathered, lowrank_factor_first, preferred_element_type=jnp...  9.72 us
  transfers between devices with their start and end apart: 4, of which 2 were waited for; matrix products, arithmetic and copies ran while one was open for 5% of the time, Pallas kernels for 0%

profile of v1, /device:TPU:1, one launch (start us, length us, event | category | flops | bytes accessed | tf_op | source)
XLA Modules:
  0.0 459.5 jit_solution(17521848172262888403)
XLA Ops:
  0.6 0.0 copy-start
  0.6 1.3 fusion.12
  2.0 1.5 fusion.27
  3.5 0.7 reshape.76
  4.2 5.0 %all-to-all-start.2 = ((f32[4,1,1024]{2,1,0:T(1,128)}), f32[4,1,1024]{2,1,0:T(1,128)S(1)}, u32[]{:S(2)}, u32[]{:S(2)}) async-start(f32[4,1,1024]{2,1,0:T(1,128)} %reshape.76), calls=%async_computation.2 | async-start | bytes 32768 | tf_op jit(solution)/shard_map/all_to_all | solution.py:23
  9.2 1.7 copy_bitcast_fusion
  10.9 2.5 all-to-all-done.2
  13.4 13.6 %all-to-all-start.4 = ((bf16[16,64,128]{2,0,1:T(8,128)(2,1)}), bf16[16,64,128]{2,0,1:T(8,128)(2,1)S(1)}, u32[]{:S(2)}, u32[]{:S(2)}) async-start(bf16[16,64,128]{2,0,1:T(8,128)(2,1)} %copy_bitcast_fusion), calls=%async_computation.4 | async-start | bytes 524288 | tf_op jit(solution)/shard_map/all_to_all | solution.py:57
  27.0 0.6 broadcast.33
  27.6 0.7 reduce.2
  28.3 0.1 reshape.77
  28.5 0.3 reshape.78
  28.8 10.2 %all-to-all-done.4 = bf16[16,64,128]{2,0,1:T(8,128)(2,1)S(1)} async-done(((bf16[16,64,128]{2,0,1:T(8,128)(2,1)}), bf16[16,64,128]{2,0,1:T(8,128)(2,1)S(1)}, u32[]{:S(2)}, u32[]{:S(2)}) %all-to-all-start.4) | async-done | bytes 262176 | tf_op jit(solution)/shard_map/all_to_all | solution.py:57
  39.0 17.9 %all_to_all.36 = f32[64,1,1024]{2,1,0:T(1,128)} all-to-all(f32[64,1,1024]{2,1,0:T(1,128)S(1)} %reshape.78), channel_id=1, replica_groups=mesh['dp_0'=4,'dp_1'=8,'dp_2'=2,'tensor'=4] {'dp_0','dp_1','dp_2'}, dimensions={0} | all-to-all | bytes 524288 | tf_op jit(solution)/shard_map/all_to_all | solution.py:23
  56.9 7.0 %stack.8 = bf16[64,16,7168]{2,1,0:T(8,128)(2,1)} broadcast(bf16[16,7168]{1,0:T(8,128)(2,1)S(1)} %fusion.12), dimensions={1,2} | broadcast | bytes 14909440 | tf_op jit(solution)/shard_map/stack | solution.py:81
  63.9 0.0 copy-start.5
  63.9 0.0 copy-start.7
  63.9 0.0 copy-start.2
  63.9 0.0 copy-start.6
  63.9 0.0 copy-start.1
  63.9 6.3 %all-to-all-start = ((bf16[64,16,7168]{2,1,0:T(8,128)(2,1)}), bf16[64,16,7168]{2,1,0:T(8,128)(2,1)}, u32[]{:S(2)}, u32[]{:S(2)}) async-start(bf16[64,16,7168]{2,1,0:T(8,128)(2,1)} %stack.8), calls=%async_computation | async-start | bytes 29360128 | tf_op jit(solution)/shard_map/all_to_all | solution.py:80
  70.3 0.0 copy-done.5
  70.3 0.1 constant_dynamic-slice_fusion
  70.3 0.5 fusion.23
  72.2 0.0 copy-done.7
  72.2 0.6 dynamic-slice.2
  72.8 0.0 copy-done.2
  72.8 1.6 convolution_convert_fusion
  74.4 35.5 %all-gather = bf16[64,64]{1,0:T(8,128)(2,1)S(1)} all-gather(bf16[16,64]{1,0:T(8,128)(2,1)S(1)} %convolution_convert_fusion), channel_id=2, replica_groups=mesh['dp_0'=4,'dp_1'=8,'dp_2'=2,'tensor'=4] {'dp_0'}, dimensions={0}, use_global_device_ids=true | all-gather | bytes 10240 | tf_op jit(solution)/shard_map/all_gather | solution.py:45
  109.9 291.9 %all-gather.1 = bf16[32,16,64]{2,1,0:T(8,128)(2,1)S(1)} all-gather(bf16[4,16,64]{2,1,0:T(8,128)(2,1)S(1)} %bitcast.66), channel_id=3, replica_groups=mesh['dp_0'=4,'dp_1'=8,'dp_2'=2,'tensor'=4] {'dp_1'}, dimensions={0}, use_global_device_ids=true | all-gather | bytes 73728 | tf_op jit(solution)/shard_map/all_gather | solution.py:45
  401.7 8.0 %all-gather.2 = bf16[16,4,16,64]{3,2,1,0:T(8,128)(2,1)S(1)} all-gather(bf16[8,4,16,64]{3,2,1,0:T(8,128)(2,1)S(1)} %bitcast.64), channel_id=4, replica_groups=mesh['dp_0'=4,'dp_1'=8,'dp_2'=2,'tensor'=4] {'dp_2'}, dimensions={0}, use_global_device_ids=true | all-gather | bytes 196608 | tf_op jit(solution)/shard_map/all_gather | solution.py:45
  409.7 0.0 copy-done.6
  409.8 0.2 compare_reduce_fusion
  410.0 0.7 fusion.17
  410.6 0.9 bitcast_convert_fusion
  411.5 2.2 reduce.3
  413.7 0.9 reshape.79
  414.7 0.0 copy-start.4
  414.7 2.3 convolution_bitcast_fusion.1
  417.0 0.0 all-to-all-done
  417.0 0.0 copy-done.1
  417.0 9.7 %fusion.25 = f32[1024,64]{0,1:T(8,128)S(1)} fusion(bf16[1024,7168]{1,0:T(8,128)(2,1)} %bitcast, bf16[7168,64]{0,1:T(8,128)(2,1)S(1)} %copy-done.1), kind=kOutput, calls=%fused_computation.41 | convolution fusion | flops 939524096 | bytes 15859712 | tf_op jit(solution)/shard_map/dot_general | solution.py:108
  426.7 1.1 dynamic-slice_bitcast_fusion.1
  427.8 0.0 copy-done.4
  427.8 0.3 convolution_bitcast_fusion
  428.1 7.5 %fusion.2 = f32[1,1024,128]{2,0,1:T(1,128)S(1)} fusion(f32[1024,2,128]{2,0,1:T(8,128)S(1)} %convolution_bitcast_fusion, pred[2]{0:T(512)(128)(4,1)S(1)} %compare_reduce_fusion, s32[1]{0:T(128)} %dynamic-slice.2), kind=kOutput, calls=%fused_computation.8 | convolution fusion | flops 3145734 | bytes 1572870 | tf_op jit(solution)/shard_map/tkd,kn->tnd/dot_general | solution.py:113
  435.5 0.0 copy-done
  435.5 7.2 %fusion.24 = f32[1024,128]{1,0:T(8,128)S(1)} fusion(bf16[1024,7168]{1,0:T(8,128)(2,1)} %bitcast, bf16[7168,128]{1,0:T(8,128)(2,1)S(1)} %copy-done), kind=kOutput, calls=%fused_computation.40 | convolution fusion | flops 1879048192 | bytes 17039360 | tf_op jit(solution)/shard_map/dot_general | solution.py:107
  442.8 2.1 fusion
  444.9 3.7 all-to-all-start.1
  448.6 0.0 copy-start.3
  448.6 9.2 %fusion.26 = f32[7168,64]{0,1:T(8,128)} fusion(bf16[1024,7168]{1,0:T(8,128)(2,1)} %bitcast, bf16[1024,64]{1,0:T(8,128)(2,1)S(1)} %bitcast.62), kind=kOutput, calls=%fused_computation.42 | convolution fusion | flops 939524096 | bytes 16646144 | tf_op jit(solution)/shard_map/dot_general | solution.py:143
  457.8 0.0 copy-done.3
  457.8 1.0 fusion.1
  458.9 0.0 all-to-all-done.1
  458.9 0.7 reduce_sum.18
  (5 shorter events, 0.1 us)
Async XLA Ops:
  0.6 434.9 %copy-start = (bf16[7168,128]{1,0:T(8,128)(2,1)S(1)}, bf16[7168,128]{1,0:T(8,128)(2,1)}, u32[]{:S(2)}) copy-start(bf16[7168,128]{1,0:T(8,128)(2,1)} %param.13) | copy-start | bytes 5505028
  4.2 9.2 %all-to-all-start.2 = ((f32[4,1,1024]{2,1,0:T(1,128)}), f32[4,1,1024]{2,1,0:T(1,128)S(1)}, u32[]{:S(2)}, u32[]{:S(2)}) async-start(f32[4,1,1024]{2,1,0:T(1,128)} %reshape.76), calls=%async_computation.2 | async-start | bytes 32768 | tf_op jit(solution)/shard_map/all_to_all | solution.py:23
  13.4 25.6 %all-to-all-start.4 = ((bf16[16,64,128]{2,0,1:T(8,128)(2,1)}), bf16[16,64,128]{2,0,1:T(8,128)(2,1)S(1)}, u32[]{:S(2)}, u32[]{:S(2)}) async-start(bf16[16,64,128]{2,0,1:T(8,128)(2,1)} %copy_bitcast_fusion), calls=%async_computation.4 | async-start | bytes 524288 | tf_op jit(solution)/shard_map/all_to_all | solution.py:57
  63.9 6.4 %copy-start.5 = (s32[64,1,2]{0,2,1:T(2,128)S(1)}, s32[64,1,2]{0,2,1:T(2,128)}, u32[]{:S(2)}) copy-start(s32[64,1,2]{0,2,1:T(2,128)} %param.17) | copy-start | bytes 1540
  63.9 8.3 %copy-start.7 = (s32[64,1]{0,1:T(1,128)S(1)}, s32[64,1]{0,1:T(1,128)}, u32[]{:S(2)}) copy-start(s32[64,1]{0,1:T(1,128)} %param.19) | copy-start | bytes 772
  63.9 8.9 %copy-start.2 = (bf16[16,8192]{1,0:T(8,128)(2,1)S(1)}, bf16[16,8192]{1,0:T(8,128)(2,1)}, u32[]{:S(2)}) copy-start(bf16[16,8192]{1,0:T(8,128)(2,1)} %param.12) | copy-start | bytes 786436
  63.9 345.9 %copy-start.6 = (s32[64,1,2]{0,2,1:T(2,128)S(1)}, s32[64,1,2]{0,2,1:T(2,128)}, u32[]{:S(2)}) copy-start(s32[64,1,2]{0,2,1:T(2,128)} %param.18) | copy-start | bytes 1540
  63.9 353.1 %copy-start.1 = (bf16[7168,64]{0,1:T(8,128)(2,1)S(1)}, bf16[7168,64]{0,1:T(8,128)(2,1)}, u32[]{:S(2)}) copy-start(bf16[7168,64]{0,1:T(8,128)(2,1)} %param.14) | copy-start | bytes 2752516
  63.9 353.1 %all-to-all-start = ((bf16[64,16,7168]{2,1,0:T(8,128)(2,1)}), bf16[64,16,7168]{2,1,0:T(8,128)(2,1)}, u32[]{:S(2)}, u32[]{:S(2)}) async-start(bf16[64,16,7168]{2,1,0:T(8,128)(2,1)} %stack.8), calls=%async_computation | async-start | bytes 29360128 | tf_op jit(solution)/shard_map/all_to_all | solution.py:80
  414.7 13.1 %copy-start.4 = (bf16[1,1,2,128,128]{4,3,2,1,0:T(8,128)(2,1)S(1)}, bf16[1,1,2,128,128]{4,3,2,1,0:T(8,128)(2,1)}, u32[]{:S(2)}) copy-start(bf16[1,1,2,128,128]{4,3,2,1,0:T(8,128)(2,1)} %param.16) | copy-start | bytes 196612
  444.9 13.9 %all-to-all-start.1 = ((f32[4,256,128]{2,1,0:T(8,128)}), f32[4,256,128]{2,1,0:T(8,128)S(1)}, u32[]{:S(2)}, u32[]{:S(2)}) async-start(f32[4,256,128]{2,1,0:T(8,128)} %bitcast.13), calls=%async_computation.1 | async-start | bytes 1048576 | tf_op jit(solution)/shard_map/all_to_all | solution.py:17
  448.6 9.2 %copy-start.3 = (f32[1024,128]{1,0:T(8,128)S(1)}, f32[1024,128]{1,0:T(8,128)}, u32[]{:S(2)}) copy-start(f32[1024,128]{1,0:T(8,128)} %bitcast_convert_fusion) | copy-start | bytes 1572868
